TPU v7x, 32 devices: a whole 2x2x4 slice. The times are simulated.
32 devices in a mesh: dp: 8 (over y, x, core), seq: 4 (over z).
Axes of the slice: x: 2, y: 2, z: 4, core: 2. Of those that a mesh axis runs over, the one named last changes fastest.
Arguments:
- states: bfloat16 [4096, 1280], P(('dp', 'seq')), parts along dimension 0, may hold values from -90 to 90
- token_kind: int32 [4096], P(('dp', 'seq')), parts along dimension 0, may hold values from 0 to 3
- episode: int32 [4096], P(('dp', 'seq')), parts along dimension 0, may hold values from 0 to 3, never falling along the last dimension, each value on 1 to 384 neighbouring positions
- kind_table: bfloat16 [4, 1280], replicated, may hold values from -3 to 3
- w_qkv: bfloat16 [1280, 3072], replicated, may hold values from -0.15625 to 0.15625
- w_out: bfloat16 [1024, 1280], replicated, may hold values from -0.1875 to 0.1875
Outputs:
- attended: bfloat16 [4096, 1280], P(('dp', 'seq')), parts along dimension 0
There are 8 independent parts, one for each index of `dp`. A program takes and returns all parts, laid end to end along the dimension named above; an argument that names none is the same for every part. Nothing has to cross between parts.
All inputs are finite; a program needn't handle non-finite values.
Results may differ from a plain program's by a relative error of at most 0.0055.
The roundings to bfloat16 on the way count: a program that leaves them out, or rounds other values in their place, can miss the bound.
Values may be sent and summed in bfloat16 or wider, within the bound.
No kernel may reach another device: no remote copies, remote signals or barrier semaphores. Data moves between devices by JAX's collectives and lax.ppermute only.
A program may use at most 128 MiB of HBM per device.

v0:
```python
import math
import jax
import jax.numpy as jnp
from jax import lax
from jax.sharding import PartitionSpec as P

HEADS = 16


def absorb(
    running, queries, query_place, query_episode, key_rows, value_rows, key_place, key_episode
):
    maxima, totals, summed = running
    temper = 1.0 / math.sqrt(queries.shape[2])
    scores = (
        jnp.einsum("qhd,khd->hqk", queries, key_rows, preferred_element_type=jnp.float32) * temper
    )
    allowed = (key_place[None, :] <= query_place[:, None]) & (
        key_episode[None, :] == query_episode[:, None]
    )
    scores = jnp.where(allowed[None], scores, -1e30)
    raised = jnp.maximum(maxima, jnp.max(scores, axis=2))
    shrink = jnp.exp(maxima - raised)
    weights = jnp.where(allowed[None], jnp.exp(scores - raised[:, :, None]), 0.0)
    totals = totals * shrink + jnp.sum(weights, axis=2)
    summed = summed * shrink.T[:, :, None] + jnp.einsum(
        "hqk,khd->qhd", weights.astype(jnp.bfloat16), value_rows, preferred_element_type=jnp.float32
    )
    return (raised, totals, summed)


def sweep_keys(
    running, queries, query_place, query_episode, key_rows, value_rows, key_place, key_episode
):
    length = key_rows.shape[0]
    stride = math.gcd(length, 512)

    def visit(number, current):
        offset = number * stride
        keys_here = lax.dynamic_slice_in_dim(key_rows, offset, stride, 0)
        values_here = lax.dynamic_slice_in_dim(value_rows, offset, stride, 0)
        place_here = lax.dynamic_slice_in_dim(key_place, offset, stride, 0)
        episode_here = lax.dynamic_slice_in_dim(key_episode, offset, stride, 0)
        skipped = (place_here[0] > query_place[-1]) | (episode_here[-1] < query_episode[0])
        return lax.cond(
            skipped,
            lambda s: s,
            lambda s: absorb(
                s,
                queries,
                query_place,
                query_episode,
                keys_here,
                values_here,
                place_here,
                episode_here,
            ),
            current,
        )

    return lax.fori_loop(0, length // stride, visit, running)


def fresh_state(count, heads, head_size):
    return (
        jnp.full((heads, count), -1e30, jnp.float32),
        jnp.zeros((heads, count), jnp.float32),
        jnp.zeros((count, heads, head_size), jnp.float32),
    )


def local(states, token_kind, episode, kind_table, w_qkv, w_out):
    rows = states.shape[0]
    kinds = kind_table.shape[0]
    picked = (token_kind[:, None] == jnp.arange(kinds, dtype=jnp.int32)[None, :]).astype(
        jnp.float32
    )
    added = jnp.dot(picked, kind_table.astype(jnp.float32), precision=lax.Precision.HIGHEST)
    inputs = (states.astype(jnp.float32) + added).astype(jnp.bfloat16)
    projected = jnp.dot(inputs, w_qkv, preferred_element_type=jnp.float32).astype(jnp.bfloat16)
    inner = w_out.shape[0]
    head_size = inner // HEADS
    queries = projected[:, :inner].reshape(rows, HEADS, head_size)
    key_flat = projected[:, inner : 2 * inner]
    value_flat = projected[:, 2 * inner :]
    key_three = key_flat.reshape(rows, HEADS, head_size)
    value_three = value_flat.reshape(rows, HEADS, head_size)
    moved_q, moved_k, moved_v = (
        lax.all_to_all(queries, "seq", split_axis=1, concat_axis=0, tiled=True),
        lax.all_to_all(key_three, "seq", split_axis=1, concat_axis=0, tiled=True),
        lax.all_to_all(value_three, "seq", split_axis=1, concat_axis=0, tiled=True),
    )
    whole_episode = lax.all_gather(episode, "seq", axis=0, tiled=True)
    length = moved_q.shape[0]
    local_heads = moved_q.shape[1]
    whole_place = jnp.arange(length, dtype=jnp.int32)
    stride = math.gcd(length, 512)

    def query_block(number, written):
        offset = number * stride
        block_q = lax.dynamic_slice_in_dim(moved_q, offset, stride, 0)
        block_place = lax.dynamic_slice_in_dim(whole_place, offset, stride, 0)
        block_episode = lax.dynamic_slice_in_dim(whole_episode, offset, stride, 0)
        maxima, totals, summed = sweep_keys(
            fresh_state(stride, local_heads, head_size),
            block_q,
            block_place,
            block_episode,
            moved_k,
            moved_v,
            whole_place,
            whole_episode,
        )
        result = (summed / totals.T[:, :, None]).astype(jnp.bfloat16)
        return lax.dynamic_update_slice_in_dim(written, result, offset, 0)

    written = lax.fori_loop(
        0, length // stride, query_block, jnp.zeros((length, local_heads, head_size), jnp.bfloat16)
    )
    heads_out = lax.all_to_all(written, "seq", split_axis=0, concat_axis=1, tiled=True).reshape(
        rows, inner
    )
    return jnp.dot(heads_out, w_out, preferred_element_type=jnp.float32).astype(jnp.bfloat16)


def solution(mesh):
    placed = (P(("dp", "seq"), None), P(("dp", "seq")), P(("dp", "seq")), P(), P(), P())
    return jax.shard_map(
        local, mesh=mesh, in_specs=placed, out_specs=P(("dp", "seq"), None), check_vma=False
    )
```

profile of v0, /device:TPU:0, one launch (start us, length us, event | category | flops | bytes accessed | tf_op | source)
XLA Modules:
  0.0 70.3 jit_solution(8716372642339516466)
XLA Ops:
  0.0 0.0 copy-start
  0.0 1.4 %fusion.23 = bf16[128,1280]{1,0:T(8,128)(2,1)S(1)} fusion(bf16[4,1280]{1,0:T(4,128)(2,1)} %param.11, bf16[128,1280]{1,0:T(8,128)(2,1)} %param.8, s32[128]{0:T(128)} %param.9), kind=kOutput, calls=%fused_computation.26 | convolution fusion | flops 1802752 | bytes 666112 | tf_op jit(solution)/shard_map/dot_general | solution.py:78
  1.4 4.5 %convolution_convert_fusion = bf16[128,3072]{1,0:T(8,128)(2,1)S(1)} fusion(bf16[128,1280]{1,0:T(8,128)(2,1)S(1)} %fusion.23, bf16[1280,3072]{1,0:T(8,128)(2,1)} %param.12), kind=kOutput, calls=%fused_computation.24 | convolution fusion | flops 1007026176 | bytes 8978432 | tf_op jit(solution)/shard_map/dot_general | solution.py:80
  6.0 0.0 copy-start.2
  6.0 0.1 fusion.25
  6.1 0.8 %copy.37 = bf16[128,1024]{0,1:T(8,128)(2,1)} copy(bf16[128,1024]{1,0:T(8,128)(2,1)S(1)} %get-tuple-element.182) | data formatting | bytes 524288 | tf_op jit(solution)/shard_map/slice | solution.py:85
  6.9 6.3 %all-to-all-start.2 = ((bf16[128,16,64]{0,2,1:T(8,128)(2,1)}), bf16[128,16,64]{0,2,1:T(8,128)(2,1)S(1)}, u32[]{:S(2)}, u32[]{:S(2)}) async-start(bf16[128,16,64]{0,2,1:T(8,128)(2,1)} %bitcast.11), calls=%async_computation.2 | async-start | bytes 524288 | tf_op jit(solution)/shard_map/all_to_all | solution.py:91
  13.2 0.8 %copy.36 = bf16[128,1024]{0,1:T(8,128)(2,1)} copy(bf16[128,1024]{1,0:T(8,128)(2,1)S(1)} %get-tuple-element.183) | data formatting | bytes 524288 | tf_op jit(solution)/shard_map/slice | solution.py:84
  14.1 8.1 %all-to-all-done.2 = bf16[128,16,64]{0,2,1:T(8,128)(2,1)S(1)} async-done(((bf16[128,16,64]{0,2,1:T(8,128)(2,1)}), bf16[128,16,64]{0,2,1:T(8,128)(2,1)S(1)}, u32[]{:S(2)}, u32[]{:S(2)}) %all-to-all-start.2) | async-done | bytes 262176 | tf_op jit(solution)/shard_map/all_to_all | solution.py:91
  22.2 3.4 %all-to-all-start.1 = ((bf16[128,16,64]{0,2,1:T(8,128)(2,1)}), bf16[128,16,64]{0,2,1:T(8,128)(2,1)S(1)}, u32[]{:S(2)}, u32[]{:S(2)}) async-start(bf16[128,16,64]{0,2,1:T(8,128)(2,1)} %bitcast.8), calls=%async_computation.1 | async-start | bytes 524288 | tf_op jit(solution)/shard_map/all_to_all | solution.py:90
  25.6 0.8 %copy.35 = bf16[128,1024]{0,1:T(8,128)(2,1)} copy(bf16[128,1024]{1,0:T(8,128)(2,1)S(1)} %get-tuple-element.184) | data formatting | bytes 524288 | tf_op jit(solution)/shard_map/slice | solution.py:83
  26.4 6.2 %all-to-all-done.1 = bf16[128,16,64]{0,2,1:T(8,128)(2,1)S(1)} async-done(((bf16[128,16,64]{0,2,1:T(8,128)(2,1)}), bf16[128,16,64]{0,2,1:T(8,128)(2,1)S(1)}, u32[]{:S(2)}, u32[]{:S(2)}) %all-to-all-start.1) | async-done | bytes 262176 | tf_op jit(solution)/shard_map/all_to_all | solution.py:90
  32.6 0.0 copy-start.1
  32.6 4.0 %all-to-all-start = ((bf16[128,16,64]{0,2,1:T(8,128)(2,1)}), bf16[128,16,64]{0,2,1:T(8,128)(2,1)}, u32[]{:S(2)}, u32[]{:S(2)}) async-start(bf16[128,16,64]{0,2,1:T(8,128)(2,1)} %bitcast.5), calls=%async_computation | async-start | bytes 524288 | tf_op jit(solution)/shard_map/all_to_all | solution.py:89
  36.6 0.0 copy-done.2
  36.6 11.3 %all-gather = s32[4,1,128]{2,1,0:T(1,128)S(1)} all-gather(s32[1,1,128]{2,1,0:T(1,128)S(1)} %bitcast.64), channel_id=1, replica_groups=mesh['dp'=8,'seq'=4] {'seq'}, dimensions={0}, use_global_device_ids=true | all-gather | bytes 2560 | tf_op jit(solution)/shard_map/all_gather | solution.py:93
  47.9 0.6 fusion.26
  49.8 0.6 fusion.27
  51.7 0.0 copy-done.1
  51.7 0.1 broadcast.75
  51.8 0.0 all-to-all-done
  51.8 4.7 %conditional.1 = ((f32[4,512]{1,0:T(4,128)S(1)}, f32[512,4,64]{0,2,1:T(8,128)S(1)})) conditional(s32[]{:T(128)} %bitcast.4, (s32[512]{0:T(512)S(1)}, s32[512]{0:T(512)S(1)}, bf16[4,128,4,64]{1,3,2,0:T(8,128)(2,1)}, bf16[4,128,4,64]{1,3,2,0:T(8,128)(2,1)}, f32[4,512]{1,0:T(4,128)S(1)}, /*index=5*/f32[512,4,64]{0,2,1:T(8,128)S(1)}, ...), branch_computations={%region_0.3_spmd, %region_3.4_spmd} | conditional | flops 283121664 | bytes 15568920 | solution.py:45
  51.8 0.3 compare_and_fusion
  52.1 1.9 %fusion = (f32[4,512]{1,0:T(4,128)S(1)}, f32[4,512,512]{1,2,0:T(8,128)S(1)}) fusion(pred[512,512]{0,1:T(8,128)(4,1)S(1)} %compare_and_fusion, bf16[4,128,4,64]{1,3,2,0:T(8,128)(2,1)} %get-tuple-element.174, bf16[4,128,4,64]{1,3,2,0:T(8,128)(2,1)} %get-tuple-element.173), kind=kOutput, calls=%fused_computation.2 | convolution fusion | flops 137361408 | bytes 4988928 | tf_op jit(solution)/shard_map/while/body/eval_jaxpr/while/body/eval_jaxpr/cond/branch_0_fun/qhd,khd->hqk/dot_general | solution.py:16
  54.0 1.0 %fusion.2 = f32[4,512]{1,0:T(4,128)S(1)} fusion(f32[4,512,512]{1,2,0:T(8,128)S(1)} %get-tuple-element.181, f32[4,512]{1,0:T(4,128)S(1)} %broadcast_maximum_fusion, pred[512,512]{0,1:T(8,128)(4,1)S(1)} %compare_and_fusion), kind=kLoop, calls=%fused_computation.4 | loop fusion | flops 5240832 | bytes 4472832 | tf_op jit(solution)/shard_map/while/body/eval_jaxpr/while/body/eval_jaxpr/cond/branch_0_fun/reduce_sum | solution.py:25
  55.1 1.4 %fusion.9 = f32[512,4,64]{0,2,1:T(8,128)S(1)} fusion(f32[4,512,512]{1,2,0:T(8,128)S(1)} %get-tuple-element.181, f32[4,512]{1,0:T(4,128)S(1)} %broadcast_maximum_fusion, pred[512,512]{0,1:T(8,128)(4,1)S(1)} %compare_and_fusion, f32[512,4,64]{0,2,1:T(8,128)S(1)} %get-tuple-element.144, f32[512,4]{0,1:T(4,128)S(1)} %get-tuple-element.178, ...), kind=kOutput, calls=%fused_computation.8 | convolution fusion | flops 139722752 | bytes 5783552 | tf_op jit(solution)/shard_map/while/body/eval_jaxpr/while/body/eval_jaxpr/cond/branch_0_fun/hqk,khd->qhd/dot_general | solution.py:26
  56.5 0.1 divide_convert_fusion
  56.5 0.3 copy.41
  56.9 0.4 reshape.84
  57.3 10.2 %all_to_all.72 = bf16[4,2,16384]{2,1,0:T(2,128)(2,1)} all-to-all(bf16[4,2,16384]{2,1,0:T(2,128)(2,1)S(1)} %reshape.84), channel_id=1, replica_groups=mesh['dp'=8,'seq'=4] {'seq'}, dimensions={0} | all-to-all | bytes 524288 | tf_op jit(solution)/shard_map/all_to_all | solution.py:120
  67.4 1.3 %reshape.85 = bf16[512,4,64]{2,1,0:T(4,128)(2,1)S(1)} reshape(bf16[4,2,16384]{2,1,0:T(2,128)(2,1)} %all_to_all.72) | data formatting | bytes 524288
  68.8 0.3 copy.43
  69.0 0.0 copy-done
  69.1 1.3 %convolution_convert_fusion.1 = bf16[128,1280]{1,0:T(8,128)(2,1)} fusion(bf16[128,1024]{0,1:T(8,128)(2,1)S(1)} %bitcast.58, bf16[1024,1280]{1,0:T(8,128)(2,1)S(1)} %copy-done), kind=kOutput, calls=%fused_computation.27 | convolution fusion | flops 335708160 | bytes 3211264 | tf_op jit(solution)/shard_map/dot_general | solution.py:123
  (5 shorter events, 0.0 us)
Async XLA Ops:
  0.0 69.0 %copy-start = (bf16[1024,1280]{1,0:T(8,128)(2,1)S(1)}, bf16[1024,1280]{1,0:T(8,128)(2,1)}, u32[]{:S(2)}) copy-start(bf16[1024,1280]{1,0:T(8,128)(2,1)} %param.13) | copy-start | bytes 7864324
  6.0 30.6 %copy-start.2 = (s32[128]{0:T(128)S(1)}, s32[128]{0:T(128)}, u32[]{:S(2)}) copy-start(s32[128]{0:T(128)} %param.10) | copy-start | bytes 1540
  6.9 15.3 %all-to-all-start.2 = ((bf16[128,16,64]{0,2,1:T(8,128)(2,1)}), bf16[128,16,64]{0,2,1:T(8,128)(2,1)S(1)}, u32[]{:S(2)}, u32[]{:S(2)}) async-start(bf16[128,16,64]{0,2,1:T(8,128)(2,1)} %bitcast.11), calls=%async_computation.2 | async-start | bytes 524288 | tf_op jit(solution)/shard_map/all_to_all | solution.py:91
  22.2 10.4 %all-to-all-start.1 = ((bf16[128,16,64]{0,2,1:T(8,128)(2,1)}), bf16[128,16,64]{0,2,1:T(8,128)(2,1)S(1)}, u32[]{:S(2)}, u32[]{:S(2)}) async-start(bf16[128,16,64]{0,2,1:T(8,128)(2,1)} %bitcast.8), calls=%async_computation.1 | async-start | bytes 524288 | tf_op jit(solution)/shard_map/all_to_all | solution.py:90
  32.6 19.1 %copy-start.1 = (bf16[128,16,64]{0,2,1:T(8,128)(2,1)}, bf16[128,16,64]{0,2,1:T(8,128)(2,1)S(1)}, u32[]{:S(2)}) copy-start(bf16[128,16,64]{0,2,1:T(8,128)(2,1)S(1)} %all-to-all-done.1) | copy-start | bytes 786436
  32.6 19.2 %all-to-all-start = ((bf16[128,16,64]{0,2,1:T(8,128)(2,1)}), bf16[128,16,64]{0,2,1:T(8,128)(2,1)}, u32[]{:S(2)}, u32[]{:S(2)}) async-start(bf16[128,16,64]{0,2,1:T(8,128)(2,1)} %bitcast.5), calls=%async_computation | async-start | bytes 524288 | tf_op jit(solution)/shard_map/all_to_all | solution.py:89
where the time goes:
time: 70.9 us; the launch traced here: 70.3 us
  blocking collectives  21.5 us (30%)
  waiting for transfers between devices  14.2 us (20%)
  starting transfers between devices  13.8 us (19%)
  matrix products  10.5 us (15%)
  local copies, waits for them, and re-layouts  6.16 us (9%)
  between operations  2.67 us (4%)
  other arithmetic  1.4 us (2%)
    all_gather x1, blocking collectives, local(): whole_episode = lax.all_gather(episode, 'seq', axis=0, tiled=True)  11.3 us
    all_to_all x1, blocking collectives, local(): lax.all_to_all(written, 'seq', split_axis=0, concat_axis=1, tiled=True)  10.2 us
    all_to_all x1, waiting for transfers between devices, local(): lax.all_to_all(value_three, 'seq', split_axis=1, concat_axis=0, tiled=True)  8.07 us
    all_to_all x1, starting transfers between devices, local(): lax.all_to_all(value_three, 'seq', split_axis=1, concat_axis=0, tiled=True)  6.35 us
    all_to_all x1, waiting for transfers between devices, local(): lax.all_to_all(key_three, 'seq', split_axis=1, concat_axis=0, tiled=True)  6.16 us
    dot_general x1, matrix products, local(): jnp.dot(inputs, w_qkv, preferred_element_type=jnp.float32)  4.53 us
    all_to_all x1, starting transfers between devices, local(): lax.all_to_all(queries, 'seq', split_axis=1, concat_axis=0, tiled=True)  4.04 us
    all_to_all x1, starting transfers between devices, local(): lax.all_to_all(key_three, 'seq', split_axis=1, concat_axis=0, tiled=True)  3.4 us
  transfers between devices with their start and end apart: 3, of which 2 were waited for; matrix products, arithmetic and copies ran while one was open for 4% of the time, Pallas kernels for 0%

commit v1 on v0

--- a/solution.py
+++ b/solution.py
@@ -117,9 +117,10 @@
     written = lax.fori_loop(
         0, length // stride, query_block, jnp.zeros((length, local_heads, head_size), jnp.bfloat16)
     )
-    heads_out = lax.all_to_all(written, "seq", split_axis=0, concat_axis=1, tiled=True).reshape(
-        rows, inner
-    )
+    heads_out = jnp.concatenate(
+        lax.all_to_all(jnp.stack(jnp.split(written, lax.axis_size("seq"), axis=0)), "seq", 0, 0),
+        axis=1,
+    ).reshape(rows, inner)
     return jnp.dot(heads_out, w_out, preferred_element_type=jnp.float32).astype(jnp.bfloat16)
 
 

time: 70.9 us -> 68.1 us (0.961)
  local copies, waits for them, and re-layouts: 6.16 us -> 3.95 us
    unnamed x8 -> x6, local copies, waits for them, and re-layouts: 1.74 us -> 0.01 us
where the time goes in v1:
time: 68.1 us; the launch traced here: 67.6 us
  blocking collectives  20.8 us (31%)
  waiting for transfers between devices  14.2 us (21%)
  starting transfers between devices  13.8 us (20%)
  matrix products  10.5 us (15%)
  local copies, waits for them, and re-layouts  3.95 us (6%)
  between operations  2.74 us (4%)
  other arithmetic  1.43 us (2%)
    all_gather x1, blocking collectives, local(): whole_episode = lax.all_gather(episode, 'seq', axis=0, tiled=True)  11.3 us
    all_to_all x1, blocking collectives, local(): lax.all_to_all(jnp.stack(jnp.split(written, lax.axis_size('seq'), axis=0)...  9.51 us
    all_to_all x1, waiting for transfers between devices, local(): lax.all_to_all(value_three, 'seq', split_axis=1, concat_axis=0, tiled=True)  8.07 us
    all_to_all x1, starting transfers between devices, local(): lax.all_to_all(value_three, 'seq', split_axis=1, concat_axis=0, tiled=True)  6.35 us
    all_to_all x1, waiting for transfers between devices, local(): lax.all_to_all(key_three, 'seq', split_axis=1, concat_axis=0, tiled=True)  6.16 us
    dot_general x1, matrix products, local(): jnp.dot(inputs, w_qkv, preferred_element_type=jnp.float32)  4.53 us
    all_to_all x1, starting transfers between devices, local(): lax.all_to_all(queries, 'seq', split_axis=1, concat_axis=0, tiled=True)  4.05 us
    all_to_all x1, starting transfers between devices, local(): lax.all_to_all(key_three, 'seq', split_axis=1, concat_axis=0, tiled=True)  3.4 us
  transfers between devices with their start and end apart: 3, of which 2 were waited for; matrix products, arithmetic and copies ran while one was open for 4% of the time, Pallas kernels for 0%

profile of v1, /device:TPU:0, one launch (start us, length us, event | category | flops | bytes accessed | tf_op | source)
XLA Modules:
  0.0 67.6 jit_solution(10843802326198403439)
XLA Ops:
  0.0 0.0 copy-start
  0.0 1.4 %fusion.23 = bf16[128,1280]{1,0:T(8,128)(2,1)S(1)} fusion(bf16[4,1280]{1,0:T(4,128)(2,1)} %param.11, bf16[128,1280]{1,0:T(8,128)(2,1)} %param.8, s32[128]{0:T(128)} %param.9), kind=kOutput, calls=%fused_computation.26 | convolution fusion | flops 1802752 | bytes 666112 | tf_op jit(solution)/shard_map/dot_general | solution.py:78
  1.4 4.5 %convolution_convert_fusion = bf16[128,3072]{1,0:T(8,128)(2,1)S(1)} fusion(bf16[128,1280]{1,0:T(8,128)(2,1)S(1)} %fusion.23, bf16[1280,3072]{1,0:T(8,128)(2,1)} %param.12), kind=kOutput, calls=%fused_computation.24 | convolution fusion | flops 1007026176 | bytes 8978432 | tf_op jit(solution)/shard_map/dot_general | solution.py:80
  6.0 0.0 copy-start.2
  6.0 0.1 fusion.25
  6.1 0.8 %copy.18 = bf16[128,1024]{0,1:T(8,128)(2,1)} copy(bf16[128,1024]{1,0:T(8,128)(2,1)S(1)} %get-tuple-element.168) | data formatting | bytes 524288 | tf_op jit(solution)/shard_map/slice | solution.py:85
  6.9 6.3 %all-to-all-start.2 = ((bf16[128,16,64]{0,2,1:T(8,128)(2,1)}), bf16[128,16,64]{0,2,1:T(8,128)(2,1)S(1)}, u32[]{:S(2)}, u32[]{:S(2)}) async-start(bf16[128,16,64]{0,2,1:T(8,128)(2,1)} %bitcast.11), calls=%async_computation.2 | async-start | bytes 524288 | tf_op jit(solution)/shard_map/all_to_all | solution.py:91
  13.2 0.8 %copy.17 = bf16[128,1024]{0,1:T(8,128)(2,1)} copy(bf16[128,1024]{1,0:T(8,128)(2,1)S(1)} %get-tuple-element.169) | data formatting | bytes 524288 | tf_op jit(solution)/shard_map/slice | solution.py:84
  14.1 8.1 %all-to-all-done.2 = bf16[128,16,64]{0,2,1:T(8,128)(2,1)S(1)} async-done(((bf16[128,16,64]{0,2,1:T(8,128)(2,1)}), bf16[128,16,64]{0,2,1:T(8,128)(2,1)S(1)}, u32[]{:S(2)}, u32[]{:S(2)}) %all-to-all-start.2) | async-done | bytes 262176 | tf_op jit(solution)/shard_map/all_to_all | solution.py:91
  22.2 3.4 %all-to-all-start.1 = ((bf16[128,16,64]{0,2,1:T(8,128)(2,1)}), bf16[128,16,64]{0,2,1:T(8,128)(2,1)S(1)}, u32[]{:S(2)}, u32[]{:S(2)}) async-start(bf16[128,16,64]{0,2,1:T(8,128)(2,1)} %bitcast.8), calls=%async_computation.1 | async-start | bytes 524288 | tf_op jit(solution)/shard_map/all_to_all | solution.py:90
  25.6 0.8 %copy.16 = bf16[128,1024]{0,1:T(8,128)(2,1)} copy(bf16[128,1024]{1,0:T(8,128)(2,1)S(1)} %get-tuple-element.170) | data formatting | bytes 524288 | tf_op jit(solution)/shard_map/slice | solution.py:83
  26.4 6.2 %all-to-all-done.1 = bf16[128,16,64]{0,2,1:T(8,128)(2,1)S(1)} async-done(((bf16[128,16,64]{0,2,1:T(8,128)(2,1)}), bf16[128,16,64]{0,2,1:T(8,128)(2,1)S(1)}, u32[]{:S(2)}, u32[]{:S(2)}) %all-to-all-start.1) | async-done | bytes 262176 | tf_op jit(solution)/shard_map/all_to_all | solution.py:90
  32.6 0.0 copy-start.1
  32.6 4.1 %all-to-all-start = ((bf16[128,16,64]{0,2,1:T(8,128)(2,1)}), bf16[128,16,64]{0,2,1:T(8,128)(2,1)}, u32[]{:S(2)}, u32[]{:S(2)}) async-start(bf16[128,16,64]{0,2,1:T(8,128)(2,1)} %bitcast.5), calls=%async_computation | async-start | bytes 524288 | tf_op jit(solution)/shard_map/all_to_all | solution.py:89
  36.6 0.0 copy-done.2
  36.6 11.3 %all-gather = s32[4,1,128]{2,1,0:T(1,128)S(1)} all-gather(s32[1,1,128]{2,1,0:T(1,128)S(1)} %bitcast.69), channel_id=1, replica_groups=mesh['dp'=8,'seq'=4] {'seq'}, dimensions={0}, use_global_device_ids=true | all-gather | bytes 2560 | tf_op jit(solution)/shard_map/all_gather | solution.py:93
  48.0 0.6 fusion.26
  49.9 0.6 fusion.27
  51.8 0.0 copy-done.1
  51.8 0.1 broadcast.75
  51.9 0.0 all-to-all-done
  51.9 4.7 %conditional.1 = ((f32[4,512]{1,0:T(4,128)S(1)}, f32[512,4,64]{0,2,1:T(8,128)S(1)})) conditional(s32[]{:T(128)} %bitcast.4, (s32[512]{0:T(512)S(1)}, s32[512]{0:T(512)S(1)}, bf16[4,128,4,64]{1,3,2,0:T(8,128)(2,1)}, bf16[4,128,4,64]{1,3,2,0:T(8,128)(2,1)}, f32[4,512]{1,0:T(4,128)S(1)}, /*index=5*/f32[512,4,64]{0,2,1:T(8,128)S(1)}, ...), branch_computations={%region_0.3_spmd, %region_3.4_spmd} | conditional | flops 283121664 | bytes 15568920 | solution.py:45
  51.9 0.3 compare_and_fusion
  52.2 1.9 %fusion = (f32[4,512]{1,0:T(4,128)S(1)}, f32[4,512,512]{1,2,0:T(8,128)S(1)}) fusion(pred[512,512]{0,1:T(8,128)(4,1)S(1)} %compare_and_fusion, bf16[4,128,4,64]{1,3,2,0:T(8,128)(2,1)} %get-tuple-element.160, bf16[4,128,4,64]{1,3,2,0:T(8,128)(2,1)} %get-tuple-element.159), kind=kOutput, calls=%fused_computation.2 | convolution fusion | flops 137361408 | bytes 4988928 | tf_op jit(solution)/shard_map/while/body/eval_jaxpr/while/body/eval_jaxpr/cond/branch_0_fun/qhd,khd->hqk/dot_general | solution.py:16
  54.2 1.0 %fusion.2 = f32[4,512]{1,0:T(4,128)S(1)} fusion(f32[4,512,512]{1,2,0:T(8,128)S(1)} %get-tuple-element.167, f32[4,512]{1,0:T(4,128)S(1)} %broadcast_maximum_fusion, pred[512,512]{0,1:T(8,128)(4,1)S(1)} %compare_and_fusion), kind=kLoop, calls=%fused_computation.4 | loop fusion | flops 5240832 | bytes 4472832 | tf_op jit(solution)/shard_map/while/body/eval_jaxpr/while/body/eval_jaxpr/cond/branch_0_fun/reduce_sum | solution.py:25
  55.2 1.4 %fusion.9 = f32[512,4,64]{0,2,1:T(8,128)S(1)} fusion(f32[4,512,512]{1,2,0:T(8,128)S(1)} %get-tuple-element.167, f32[4,512]{1,0:T(4,128)S(1)} %broadcast_maximum_fusion, pred[512,512]{0,1:T(8,128)(4,1)S(1)} %compare_and_fusion, f32[512,4,64]{0,2,1:T(8,128)S(1)} %get-tuple-element.144, f32[512,4]{0,1:T(4,128)S(1)} %get-tuple-element.164, ...), kind=kOutput, calls=%fused_computation.8 | convolution fusion | flops 139722752 | bytes 5783552 | tf_op jit(solution)/shard_map/while/body/eval_jaxpr/while/body/eval_jaxpr/cond/branch_0_fun/hqk,khd->qhd/dot_general | solution.py:26
  56.6 0.1 divide_convert_fusion
  56.7 0.1 slice_bitcast_fusion.3
  56.8 9.5 %all_to_all.62 = bf16[4,128,4,64]{1,3,2,0:T(8,128)(2,1)S(1)} all-to-all(bf16[4,128,4,64]{1,3,2,0:T(8,128)(2,1)S(1)} %pad_maximum_fusion), channel_id=1, replica_groups=mesh['dp'=8,'seq'=4] {'seq'}, dimensions={0} | all-to-all | bytes 524288 | tf_op jit(solution)/shard_map/all_to_all | solution.py:121
  66.3 0.0 copy-done
  66.3 1.3 %convolution_convert_fusion.1 = bf16[128,1280]{1,0:T(8,128)(2,1)} fusion(bf16[128,1024]{0,1:T(8,128)(2,1)S(1)} %bitcast.63, bf16[1024,1280]{1,0:T(8,128)(2,1)S(1)} %copy-done), kind=kOutput, calls=%fused_computation.27 | convolution fusion | flops 335708160 | bytes 3211264 | tf_op jit(solution)/shard_map/dot_general | solution.py:124
  (6 shorter events, 0.1 us)
Async XLA Ops:
  0.0 66.3 %copy-start = (bf16[1024,1280]{1,0:T(8,128)(2,1)S(1)}, bf16[1024,1280]{1,0:T(8,128)(2,1)}, u32[]{:S(2)}) copy-start(bf16[1024,1280]{1,0:T(8,128)(2,1)} %param.13) | copy-start | bytes 7864324
  6.0 30.7 %copy-start.2 = (s32[128]{0:T(128)S(1)}, s32[128]{0:T(128)}, u32[]{:S(2)}) copy-start(s32[128]{0:T(128)} %param.10) | copy-start | bytes 1540
  6.9 15.3 %all-to-all-start.2 = ((bf16[128,16,64]{0,2,1:T(8,128)(2,1)}), bf16[128,16,64]{0,2,1:T(8,128)(2,1)S(1)}, u32[]{:S(2)}, u32[]{:S(2)}) async-start(bf16[128,16,64]{0,2,1:T(8,128)(2,1)} %bitcast.11), calls=%async_computation.2 | async-start | bytes 524288 | tf_op jit(solution)/shard_map/all_to_all | solution.py:91
  22.2 10.4 %all-to-all-start.1 = ((bf16[128,16,64]{0,2,1:T(8,128)(2,1)}), bf16[128,16,64]{0,2,1:T(8,128)(2,1)S(1)}, u32[]{:S(2)}, u32[]{:S(2)}) async-start(bf16[128,16,64]{0,2,1:T(8,128)(2,1)} %bitcast.8), calls=%async_computation.1 | async-start | bytes 524288 | tf_op jit(solution)/shard_map/all_to_all | solution.py:90
  32.6 19.2 %copy-start.1 = (bf16[128,16,64]{0,2,1:T(8,128)(2,1)}, bf16[128,16,64]{0,2,1:T(8,128)(2,1)S(1)}, u32[]{:S(2)}) copy-start(bf16[128,16,64]{0,2,1:T(8,128)(2,1)S(1)} %all-to-all-done.1) | copy-start | bytes 786436
  32.6 19.3 %all-to-all-start = ((bf16[128,16,64]{0,2,1:T(8,128)(2,1)}), bf16[128,16,64]{0,2,1:T(8,128)(2,1)}, u32[]{:S(2)}, u32[]{:S(2)}) async-start(bf16[128,16,64]{0,2,1:T(8,128)(2,1)} %bitcast.5), calls=%async_computation | async-start | bytes 524288 | tf_op jit(solution)/shard_map/all_to_all | solution.py:89
